TPU v7x, 128 devices: a whole 4x4x4 slice. The times are simulated.
128 devices in a mesh: ctx: 8 (over x, z_lo), fsdp: 16 (over z_hi, y, core).
Axes of the slice: x: 4, y: 4, z: 4 (z_hi: 2, z_lo: 2; z = z_hi * 2 + z_lo), core: 2. Of those that a mesh axis runs over, the one named last changes fastest.
Arguments:
- inputs: bfloat16 [16, 1024, 1152], P('fsdp', 'ctx'), may hold values from -6 to 6
- out_grad: bfloat16 [16, 1024, 1152], P('fsdp', 'ctx'), may hold values from -6 to 6
- positions: int32 [16, 1024], P('fsdp', 'ctx'), may hold values from 0 to 1023, as said below
- block_order: int32 [8, 2], replicated, may hold values from 0 to 15, as said below
- w_query: bfloat16 [1152, 1024], P('fsdp'), may hold values from -0.1875 to 0.1875
- w_key: bfloat16 [1152, 256], P('fsdp'), may hold values from -0.1875 to 0.1875
- w_value: bfloat16 [1152, 256], P('fsdp'), may hold values from -0.1875 to 0.1875
- w_output: bfloat16 [1024, 1152], P(None, 'fsdp'), may hold values from -0.1875 to 0.1875
- w_gate: bfloat16 [6912, 1152], P('fsdp'), may hold values from -0.1875 to 0.1875
- w_up: bfloat16 [6912, 1152], P('fsdp'), may hold values from -0.1875 to 0.1875
- w_down: bfloat16 [6912, 1152], P('fsdp'), may hold values from -0.078125 to 0.078125
- gain_in: bfloat16 [1152], P('fsdp'), may hold values from 0.099609375 to 1.8984375
- gain_query: bfloat16 [256], P('fsdp'), may hold values from 0.099609375 to 1.8984375
- gain_key: bfloat16 [256], P('fsdp'), may hold values from 0.099609375 to 1.8984375
- gain_attn: bfloat16 [1152], P('fsdp'), may hold values from 0.099609375 to 1.8984375
- gain_pre: bfloat16 [1152], P('fsdp'), may hold values from 0.099609375 to 1.8984375
- gain_post: bfloat16 [1152], P('fsdp'), may hold values from 0.099609375 to 1.8984375
Outputs:
- outputs: bfloat16 [16, 1024, 1152], P('fsdp', 'ctx')
- in_grad: bfloat16 [16, 1024, 1152], P('fsdp', 'ctx')
- grad_w_query: float32 [1152, 1024], P('fsdp')
- grad_w_key: float32 [1152, 256], P('fsdp')
- grad_w_value: float32 [1152, 256], P('fsdp')
- grad_w_output: float32 [1024, 1152], P(None, 'fsdp')
- grad_w_gate: float32 [6912, 1152], P('fsdp')
- grad_w_up: float32 [6912, 1152], P('fsdp')
- grad_w_down: float32 [6912, 1152], P('fsdp')
- grad_gain_in: float32 [1152], P('fsdp')
- grad_gain_query: float32 [256], P('fsdp')
- grad_gain_key: float32 [256], P('fsdp')
- grad_gain_attn: float32 [1152], P('fsdp')
- grad_gain_pre: float32 [1152], P('fsdp')
- grad_gain_post: float32 [1152], P('fsdp')
Inputs may be any that keep to these rules, and one draw needn't show every extreme that they name: `block_order`: row c names the two blocks of 64 tokens in device c's rows, in order; every block appears once, and a row holds blocks k and m with k + m one less than the number of blocks. `positions`: each row's offset from the start of its document in the sequence; documents begin at the sequence's first token and at random places; sequence 0 is one document.
All inputs are finite; a program needn't handle non-finite values.
Results may differ from a plain program's by a relative error of at most 0.03.
Values may be sent and summed in bfloat16 or wider, within the bound.
No kernel may reach another device: no remote copies, remote signals or barrier semaphores. Data moves between devices by JAX's collectives and lax.ppermute only.
A program may use at most 128 MiB of HBM per device.

v0:
```python
import jax
import jax.numpy as jnp
from jax import lax
from jax.sharding import PartitionSpec as P

H = 4
HD = 256
EPS = 1e-06
ROPE_BASE = 1000000.0
GELU_C = 0.7978845608028654
GELU_A = 0.044715


def norm_forward(values, gain):
    inverse = lax.rsqrt(jnp.mean(values * values, axis=-1, keepdims=True) + EPS)
    unit = values * inverse
    return (unit * gain, unit, inverse)


def norm_backward(upstream, unit, inverse, gain):
    scaled = upstream * gain
    inner = jnp.mean(scaled * unit, axis=-1, keepdims=True)
    leading = tuple(range(upstream.ndim - 1))
    return (inverse * (scaled - unit * inner), jnp.sum(upstream * unit, axis=leading))


def gelu_pair(gate):
    inner = GELU_C * (gate + GELU_A * gate * gate * gate)
    tangent = jnp.tanh(inner)
    value = 0.5 * gate * (1.0 + tangent)
    slope = 0.5 * (1.0 + tangent) + 0.5 * gate * (1.0 - tangent * tangent) * GELU_C * (
        1.0 + 3.0 * GELU_A * gate * gate
    )
    return (value, slope)


def rope_tables(positions, width):
    half = width // 2
    freqs = ROPE_BASE ** (-2.0 * jnp.arange(half, dtype=jnp.float32) / width)
    angles = positions.astype(jnp.float32)[:, None] * freqs[None, :]
    return (jnp.cos(angles), jnp.sin(angles))


def rotate(values, cosine, sine):
    half = values.shape[-1] // 2
    first = values[..., :half]
    second = values[..., half:]
    return jnp.concatenate(
        [first * cosine - second * sine, second * cosine + first * sine], axis=-1
    )


def rotate_back(values, cosine, sine):
    half = values.shape[-1] // 2
    first = values[..., :half]
    second = values[..., half:]
    return jnp.concatenate(
        [first * cosine + second * sine, second * cosine - first * sine], axis=-1
    )


def sequence_rows(order_flat, first_row, count, block):
    rows = first_row + jnp.arange(count, dtype=jnp.int32)
    slots = rows // block
    table = jnp.arange(order_flat.shape[0], dtype=jnp.int32)
    picked = jnp.sum(jnp.where(slots[:, None] == table[None, :], order_flat[None, :], 0), axis=1)
    return picked * block + rows % block


def body(
    inputs,
    out_grad,
    positions,
    block_order,
    w_query,
    w_key,
    w_value,
    w_output,
    w_gate,
    w_up,
    w_down,
    gain_in,
    gain_query,
    gain_key,
    gain_attn,
    gain_pre,
    gain_post,
):
    f32 = jnp.float32
    low = jnp.bfloat16
    tokens = inputs[0]
    local = tokens.shape[0]
    parts = lax.axis_size("ctx")
    total = local * parts
    block = local // 2
    gathered = (
        lax.all_gather(w_query, "fsdp", axis=0, tiled=True),
        lax.all_gather(w_key, "fsdp", axis=0, tiled=True),
        lax.all_gather(w_value, "fsdp", axis=0, tiled=True),
        lax.all_gather(w_output, "fsdp", axis=1, tiled=True),
        lax.all_gather(gain_in, "fsdp", axis=0, tiled=True),
        lax.all_gather(gain_query, "fsdp", axis=0, tiled=True),
        lax.all_gather(gain_key, "fsdp", axis=0, tiled=True),
        lax.all_gather(gain_attn, "fsdp", axis=0, tiled=True),
        lax.all_gather(gain_pre, "fsdp", axis=0, tiled=True),
        lax.all_gather(gain_post, "fsdp", axis=0, tiled=True),
    )
    full_query, full_key, full_value, full_output = (
        gathered[0],
        gathered[1],
        gathered[2],
        gathered[3],
    )
    norm_in, norm_query, norm_key, norm_attn, norm_pre, norm_post = [
        g.astype(f32) for g in gathered[4:]
    ]
    ctx_index = lax.axis_index("ctx")
    order_flat = block_order.reshape(-1)
    my_seq = sequence_rows(order_flat, ctx_index * local, local, block)
    all_seq = sequence_rows(order_flat, 0, total, block)
    flat_in = tokens.astype(f32)
    normed_full, unit_in, inv_in = norm_forward(flat_in, norm_in)
    normed_in = normed_full.astype(low)
    queries = jnp.dot(normed_in, full_query, preferred_element_type=f32).reshape(local, H, HD)
    keys_raw = jnp.dot(normed_in, full_key, preferred_element_type=f32)
    values = jnp.dot(normed_in, full_value, preferred_element_type=f32).astype(low)
    query_normed, query_unit, query_inv = norm_forward(queries, norm_query)
    key_normed, key_unit, key_inv = norm_forward(keys_raw, norm_key)
    cosine, sine = rope_tables(positions[0], HD)
    scale = HD ** (-0.5)
    query_rot = (rotate(query_normed, cosine[:, None, :], sine[:, None, :]) * scale).astype(low)
    key_rot = rotate(key_normed, cosine, sine).astype(low)
    key_all, value_all = (
        lax.all_gather(key_rot, "ctx", axis=0, tiled=True),
        lax.all_gather(values, "ctx", axis=0, tiled=True),
    )
    scores = jnp.einsum("qhd,kd->hqk", query_rot, key_all, preferred_element_type=f32)
    allowed = my_seq[:, None] >= all_seq[None, :]
    scores = jnp.where(allowed[None], scores, -jnp.inf)
    highest = jnp.max(scores, axis=-1, keepdims=True)
    log_total = highest + jnp.log(jnp.sum(jnp.exp(scores - highest), axis=-1, keepdims=True))
    probs_full = jnp.exp(scores - log_total)
    probs = probs_full.astype(low)
    attended = (
        jnp.einsum("hqk,kd->qhd", probs, value_all, preferred_element_type=f32)
        .reshape(local, H * HD)
        .astype(low)
    )
    branch_attn = jnp.dot(attended, full_output, preferred_element_type=f32)
    attn_normed, attn_unit, attn_inv = norm_forward(branch_attn, norm_attn)
    residual = flat_in + attn_normed
    pre_full, pre_unit, pre_inv = norm_forward(residual, norm_pre)
    normed_pre = pre_full.astype(low)
    rows_all = lax.all_gather(normed_pre, "fsdp", axis=0, tiled=True)
    gate = jnp.einsum("td,fd->tf", rows_all, w_gate, preferred_element_type=f32)
    upper = jnp.einsum("td,fd->tf", rows_all, w_up, preferred_element_type=f32)
    gelu_value, gelu_slope = gelu_pair(gate)
    hidden = (gelu_value * upper).astype(low)
    branch_ffn = lax.psum_scatter(
        jnp.dot(hidden, w_down, preferred_element_type=f32).astype(jnp.bfloat16),
        "fsdp",
        scatter_dimension=0,
        tiled=True,
    ).astype(jnp.float32)
    post_normed, post_unit, post_inv = norm_forward(branch_ffn, norm_post)
    outputs = (residual + post_normed).astype(low)
    grad_out = out_grad[0].astype(f32)
    grad_ffn_full, grad_gain_post = norm_backward(grad_out, post_unit, post_inv, norm_post)
    grad_ffn = grad_ffn_full.astype(low)
    grad_all = lax.all_gather(grad_ffn, "fsdp", axis=0, tiled=True)
    grad_hidden = jnp.einsum("td,fd->tf", grad_all, w_down, preferred_element_type=f32)
    grad_gate = (grad_hidden * upper * gelu_slope).astype(low)
    grad_up = (grad_hidden * gelu_value).astype(low)
    shard_gate = jnp.einsum("tf,td->fd", grad_gate, rows_all, preferred_element_type=f32)
    shard_up = jnp.einsum("tf,td->fd", grad_up, rows_all, preferred_element_type=f32)
    shard_down = jnp.einsum("tf,td->fd", hidden, grad_all, preferred_element_type=f32)
    grad_pre = lax.psum_scatter(
        (
            jnp.dot(grad_gate, w_gate, preferred_element_type=f32)
            + jnp.dot(grad_up, w_up, preferred_element_type=f32)
        ).astype(jnp.bfloat16),
        "fsdp",
        scatter_dimension=0,
        tiled=True,
    ).astype(jnp.float32)
    grad_from_pre, grad_gain_pre = norm_backward(grad_pre, pre_unit, pre_inv, norm_pre)
    grad_residual = grad_out + grad_from_pre
    grad_branch_full, grad_gain_attn = norm_backward(grad_residual, attn_unit, attn_inv, norm_attn)
    grad_branch = grad_branch_full.astype(low)
    term_output = jnp.einsum("tc,td->cd", attended, grad_branch, preferred_element_type=f32)
    grad_attended = jnp.einsum(
        "td,cd->tc", grad_branch, full_output, preferred_element_type=f32
    ).astype(low)
    grad_heads = grad_attended.reshape(local, H, HD)
    attended_heads = attended.reshape(local, H, HD)
    delta = jnp.transpose(jnp.sum(grad_heads.astype(f32) * attended_heads.astype(f32), axis=-1))[
        :, :, None
    ]
    grad_probs = jnp.einsum("qhd,kd->hqk", grad_heads, value_all, preferred_element_type=f32)
    grad_scores = (probs_full * (grad_probs - delta)).astype(low)
    value_term = jnp.einsum("hqk,qhd->kd", probs, grad_heads, preferred_element_type=f32)
    key_term = jnp.einsum("hqk,qhd->kd", grad_scores, query_rot, preferred_element_type=f32)
    key_value_terms = jnp.concatenate([key_term, value_term], axis=1)
    grad_query_rot = jnp.einsum("hqk,kd->qhd", grad_scores, key_all, preferred_element_type=f32)
    summed_kv = lax.psum_scatter(
        key_value_terms.astype(jnp.bfloat16), "ctx", scatter_dimension=0, tiled=True
    ).astype(jnp.float32)
    grad_key_rot = summed_kv[:, :HD]
    grad_values = summed_kv[:, HD:].astype(low)
    grad_q_normed = rotate_back(grad_query_rot * scale, cosine[:, None, :], sine[:, None, :])
    grad_q_full, grad_gain_query = norm_backward(grad_q_normed, query_unit, query_inv, norm_query)
    grad_k_normed = rotate_back(grad_key_rot, cosine, sine)
    grad_k_full, grad_gain_key = norm_backward(grad_k_normed, key_unit, key_inv, norm_key)
    grad_q_in = grad_q_full.reshape(local, H * HD).astype(low)
    grad_k_in = grad_k_full.astype(low)
    term_query = jnp.einsum("td,tc->dc", normed_in, grad_q_in, preferred_element_type=f32)
    term_key = jnp.einsum("td,tc->dc", normed_in, grad_k_in, preferred_element_type=f32)
    term_value = jnp.einsum("td,tc->dc", normed_in, grad_values, preferred_element_type=f32)
    grad_normed = (
        jnp.einsum("tc,dc->td", grad_q_in, full_query, preferred_element_type=f32)
        + jnp.einsum("tc,dc->td", grad_k_in, full_key, preferred_element_type=f32)
        + jnp.einsum("tc,dc->td", grad_values, full_value, preferred_element_type=f32)
    )
    grad_from_in, grad_gain_in = norm_backward(grad_normed, unit_in, inv_in, norm_in)
    in_grad = (grad_residual + grad_from_in).astype(low)
    shards = (
        lax.psum_scatter(
            term_query.astype(jnp.bfloat16), "fsdp", scatter_dimension=0, tiled=True
        ).astype(jnp.float32),
        lax.psum_scatter(
            term_key.astype(jnp.bfloat16), "fsdp", scatter_dimension=0, tiled=True
        ).astype(jnp.float32),
        lax.psum_scatter(
            term_value.astype(jnp.bfloat16), "fsdp", scatter_dimension=0, tiled=True
        ).astype(jnp.float32),
        lax.psum_scatter(
            term_output.astype(jnp.bfloat16), "fsdp", scatter_dimension=1, tiled=True
        ).astype(jnp.float32),
        lax.psum_scatter(
            grad_gain_in.astype(jnp.bfloat16), "fsdp", scatter_dimension=0, tiled=True
        ).astype(jnp.float32),
        lax.psum_scatter(
            grad_gain_query.astype(jnp.bfloat16), "fsdp", scatter_dimension=0, tiled=True
        ).astype(jnp.float32),
        lax.psum_scatter(
            grad_gain_key.astype(jnp.bfloat16), "fsdp", scatter_dimension=0, tiled=True
        ).astype(jnp.float32),
        lax.psum_scatter(
            grad_gain_attn.astype(jnp.bfloat16), "fsdp", scatter_dimension=0, tiled=True
        ).astype(jnp.float32),
        lax.psum_scatter(
            grad_gain_pre.astype(jnp.bfloat16), "fsdp", scatter_dimension=0, tiled=True
        ).astype(jnp.float32),
        lax.psum_scatter(
            grad_gain_post.astype(jnp.bfloat16), "fsdp", scatter_dimension=0, tiled=True
        ).astype(jnp.float32),
    )
    totals = (
        lax.psum(shards[0].astype(jnp.bfloat16), "ctx").astype(jnp.float32),
        lax.psum(shards[1].astype(jnp.bfloat16), "ctx").astype(jnp.float32),
        lax.psum(shards[2].astype(jnp.bfloat16), "ctx").astype(jnp.float32),
        lax.psum(shards[3].astype(jnp.bfloat16), "ctx").astype(jnp.float32),
        lax.psum(shard_gate.astype(jnp.bfloat16), "ctx").astype(jnp.float32),
        lax.psum(shard_up.astype(jnp.bfloat16), "ctx").astype(jnp.float32),
        lax.psum(shard_down.astype(jnp.bfloat16), "ctx").astype(jnp.float32),
        lax.psum(shards[4].astype(jnp.bfloat16), "ctx").astype(jnp.float32),
        lax.psum(shards[5].astype(jnp.bfloat16), "ctx").astype(jnp.float32),
        lax.psum(shards[6].astype(jnp.bfloat16), "ctx").astype(jnp.float32),
        lax.psum(shards[7].astype(jnp.bfloat16), "ctx").astype(jnp.float32),
        lax.psum(shards[8].astype(jnp.bfloat16), "ctx").astype(jnp.float32),
        lax.psum(shards[9].astype(jnp.bfloat16), "ctx").astype(jnp.float32),
    )
    return (
        outputs[None],
        in_grad[None],
        totals[0],
        totals[1],
        totals[2],
        totals[3],
        totals[4],
        totals[5],
        totals[6],
        totals[7],
        totals[8],
        totals[9],
        totals[10],
        totals[11],
        totals[12],
    )


def solution(mesh):
    placed = (
        P("fsdp", "ctx", None),
        P("fsdp", "ctx", None),
        P("fsdp", "ctx"),
        P(),
        P("fsdp", None),
        P("fsdp", None),
        P("fsdp", None),
        P(None, "fsdp"),
        P("fsdp", None),
        P("fsdp", None),
        P("fsdp", None),
        P("fsdp"),
        P("fsdp"),
        P("fsdp"),
        P("fsdp"),
        P("fsdp"),
        P("fsdp"),
    )
    return jax.shard_map(
        body,
        mesh=mesh,
        in_specs=placed,
        out_specs=(
            P("fsdp", "ctx", None),
            P("fsdp", "ctx", None),
            P("fsdp", None),
            P("fsdp", None),
            P("fsdp", None),
            P(None, "fsdp"),
            P("fsdp", None),
            P("fsdp", None),
            P("fsdp", None),
            P("fsdp"),
            P("fsdp"),
            P("fsdp"),
            P("fsdp"),
            P("fsdp"),
            P("fsdp"),
        ),
        check_vma=False,
    )
```

profile of v0, /device:TPU:8, one launch (start us, length us, event | category | flops | bytes accessed | tf_op | source)
XLA Modules:
  0.0 1100.2 jit_solution(11387176566763124986)
XLA Ops:
  18.5 65.3 %all-reduce.13 = (bf16[1152]{0:T(1024)(128)(2,1)S(1)}, bf16[256]{0:T(256)(128)(2,1)S(1)}, bf16[256]{0:T(256)(128)(2,1)S(1)}, bf16[1152]{0:T(1024)(128)(2,1)S(1)}...) all-reduce(bf16[1152]{0:T(1024)(128)(2,1)S(1)} %dynamic-update-slic, ...), channel_id=1, replica_groups=mesh['ctx'=8,'fsdp'=16] {'fsdp'}, use_global_device_ids=true, to_apply=%add | all-reduce | flops 5120 | bytes 20480
  83.8 26.9 %all_gather.45 = bf16[1152,256]{1,0:T(8,128)(2,1)S(1)} all-gather(bf16[72,256]{1,0:T(8,128)(2,1)} %param.22), channel_id=1, replica_groups=mesh['ctx'=8,'fsdp'=16] {'fsdp'}, dimensions={0}, use_global_device_ids=true | all-gather | bytes 626688 | tf_op jit(solution)/shard_map/all_gather | solution.py:98
  113.2 29.1 %all_gather.47 = bf16[1024,256]{1,0:T(8,128)(2,1)S(1)} all-gather(bf16[128,256]{1,0:T(8,128)(2,1)S(1)} %pad_maximum_fusion.3), channel_id=1, replica_groups=mesh['ctx'=8,'fsdp'=16] {'ctx'}, dimensions={0}, use_global_device_ids=true | all-gather | bytes 589824 | tf_op jit(solution)/shard_map/all_gather | solution.py:134
  142.3 21.9 %all_gather.43 = bf16[1152,256]{1,0:T(8,128)(2,1)S(1)} all-gather(bf16[72,256]{1,0:T(8,128)(2,1)S(1)} %copy-done.39), channel_id=1, replica_groups=mesh['ctx'=8,'fsdp'=16] {'fsdp'}, dimensions={0}, use_global_device_ids=true | all-gather | bytes 626688 | tf_op jit(solution)/shard_map/all_gather | solution.py:99
  165.3 29.2 %all_gather.44 = bf16[1024,256]{1,0:T(8,128)(2,1)S(1)} all-gather(bf16[128,256]{1,0:T(8,128)(2,1)S(1)} %convolution_convert_fusion.10), channel_id=1, replica_groups=mesh['ctx'=8,'fsdp'=16] {'ctx'}, dimensions={0}, use_global_device_ids=true | all-gather | bytes 589824 | tf_op jit(solution)/shard_map/all_gather | solution.py:135
  194.6 4.5 copy.77
  199.0 2.6 multiply_reduce_fusion.7
  205.1 2.7 multiply_reduce_fusion.3
  209.2 55.1 %all-gather.9.cloned.1.call-done = bf16[2048,1152]{1,0:T(8,128)(2,1)} async-done(((bf16[128,1152]{1,0:T(8,128)(2,1)}), bf16[2048,1152]{1,0:T(8,128)(2,1)}) %all-gather.9.cloned.1.call-update) | async-done | bytes 4718608 | tf_op jit(solution)/shard_map/all_gather | solution.py:154
  264.3 5.2 fusion.102
  269.6 4.6 multiply_convert_fusion.1
  275.5 4.6 convolution_convert_fusion
  280.2 81.5 %reduce-scatter.8.cloned.1.call-done = bf16[128,1152]{1,0:T(8,128)(2,1)} async-done(((bf16[2048,1152]{1,0:T(8,128)(2,1)}), bf16[128,1152]{1,0:T(8,128)(2,1)}) %reduce-scatter.8.cloned.1.call-update) | async-done | bytes 294928 | tf_op jit(solution)/shard_map/reduce_scatter | solution.py:159
  366.3 56.5 %all-gather.11.cloned.1.call-done = bf16[2048,1152]{1,0:T(8,128)(2,1)} async-done(((bf16[128,1152]{1,0:T(8,128)(2,1)}), bf16[2048,1152]{1,0:T(8,128)(2,1)}) %all-gather.11.cloned.1.call-update) | async-done | bytes 4718608 | tf_op jit(solution)/shard_map/all_gather | solution.py:170
  422.8 8.5 multiply_convert_fusion
  431.4 3.0 fusion.103
  434.4 4.6 add_convert_fusion
  439.1 81.6 %reduce-scatter.10.cloned.1.call-done = bf16[128,1152]{1,0:T(8,128)(2,1)} async-done(((bf16[2048,1152]{1,0:T(8,128)(2,1)}), bf16[128,1152]{1,0:T(8,128)(2,1)}) %reduce-scatter.10.cloned.1.call-update) | async-done | bytes 294928 | tf_op jit(solution)/shard_map/reduce_scatter | solution.py:177
  522.0 2.3 multiply_reduce_fusion
  533.6 38.6 %reduce-scatter.12.cloned.1.call-done = bf16[128,512]{1,0:T(8,128)(2,1)} async-done(((bf16[1024,512]{1,0:T(8,128)(2,1)}), bf16[128,512]{1,0:T(8,128)(2,1)}) %reduce-scatter.12.cloned.1.call-update) | async-done | bytes 131088 | tf_op jit(solution)/shard_map/reduce_scatter | solution.py:205
  577.3 2.2 convolution_convert_fusion.1
  581.4 2.4 convolution_convert_fusion.2
  585.2 6.5 convolution_convert_fusion.3
  591.7 3.4 convolution_convert_fusion.4
  597.0 60.0 %all-reduce.12 = (bf16[1152]{0:T(1024)(128)(2,1)S(1)}, bf16[256]{0:T(256)(128)(2,1)S(1)}, bf16[256]{0:T(256)(128)(2,1)S(1)}, bf16[1152]{0:T(1024)(128)(2,1)S(1)}...) all-reduce(bf16[1152]{0:T(1024)(128)(2,1)S(1)} %get-tuple-element.2, ...), channel_id=9, replica_groups=mesh['ctx'=8,'fsdp'=16] {'fsdp'}, use_global_device_ids=true, to_apply=%region_32.33.clone | all-reduce | flops 5120 | bytes 20480
  660.5 45.4 %reduce-scatter.16.cloned.1.call-done = bf16[72,256]{1,0:T(8,128)(2,1)} async-done(((bf16[1152,256]{1,0:T(8,128)(2,1)}), bf16[72,256]{1,0:T(8,128)(2,1)}) %reduce-scatter.16.cloned.1.call-update) | async-done | bytes 36880 | tf_op jit(solution)/shard_map/reduce_scatter | solution.py:230
  706.0 6.3 convolution_convert_fusion.5
  712.3 68.7 %reduce-scatter.20.cloned.1.call-done = bf16[1024,72]{0,1:T(8,128)(2,1)} async-done(((bf16[1024,1152]{0,1:T(8,128)(2,1)}), bf16[1024,72]{0,1:T(8,128)(2,1)}) %reduce-scatter.20.cloned.1.call-update) | async-done | bytes 147472 | tf_op jit(solution)/shard_map/reduce_scatter | solution.py:236
  781.0 75.3 %reduce-scatter.14.cloned.1.call-done = bf16[72,1024]{1,0:T(8,128)(2,1)} async-done(((bf16[1152,1024]{1,0:T(8,128)(2,1)}), bf16[72,1024]{1,0:T(8,128)(2,1)}) %reduce-scatter.14.cloned.1.call-update) | async-done | bytes 147472 | tf_op jit(solution)/shard_map/reduce_scatter | solution.py:227
  857.3 71.0 %all-reduce.19.cloned.1.call-done = (bf16[72,256]{1,0:T(8,128)(2,1)}, bf16[72,256]{1,0:T(8,128)(2,1)}, bf16[72]{0:T(256)(128)(2,1)}, bf16[16]{0:T(256)(128)(2,1)...) async-done(((bf16[72,256]{1,0:T(8,128)(2,1)}, bf16[72,256]{1,0:T(8,128)(2,1)}, bf16[72]{0:T(256)(128)(2,1)}, ...) | async-done | bytes 74384 | tf_op jit(solution)/shard_map/psum | solution.py:260
  938.0 146.8 %all-reduce.21.cloned.1.call-done = (bf16[72,1024]{1,0:T(8,128)(2,1)}, bf16[1024,72]{0,1:T(8,128)(2,1)}, bf16[432,1152]{1,0:T(8,128)(2,1)}, bf16[432,1152]{1,0:T(8,128)(2,1)}, bf16[432,1152]{1,0:T(8,128)(2,1)}) async-done(((bf16[72,1024]{1,0:T(8,128)(2,1)}, bf16[1024,72]{0,1:T(8,128)(2,1)}, bf16[432,1152]{1,0:T(8,128)(2,1)}, bf16[432,1152]{1,0:T(8,128)(2,1)}, bf16[432,1152]{1,0:T(8,128)(2,1)}), ...) | async-done | bytes 3280912 | tf_op jit(solution)/shard_map/psum | solution.py:259
  1088.1 2.7 convert_element_type.287
  (243 shorter events, 63.4 us)
Async XLA Ops:
  7.2 268.3 %copy-start = (bf16[432,1152]{1,0:T(8,128)(2,1)S(1)}, bf16[432,1152]{1,0:T(8,128)(2,1)}, u32[]{:S(2)}) copy-start(bf16[432,1152]{1,0:T(8,128)(2,1)} %param.27) | copy-start | bytes 2985988
  7.2 157.8 %copy-start.2 = (bf16[1,128,1152]{2,1,0:T(8,128)(2,1)S(1)}, bf16[1,128,1152]{2,1,0:T(8,128)(2,1)}, u32[]{:S(2)}) copy-start(bf16[1,128,1152]{2,1,0:T(8,128)(2,1)} %param.17) | copy-start | bytes 884740
  7.2 105.3 %copy-start.48 = (s32[1,128]{1,0:T(1,128)S(1)}, s32[1,128]{1,0:T(1,128)}, u32[]{:S(2)}) copy-start(s32[1,128]{1,0:T(1,128)} %param.19) | copy-start | bytes 1540
  7.2 135.1 %copy-start.39 = (bf16[72,256]{1,0:T(8,128)(2,1)S(1)}, bf16[72,256]{1,0:T(8,128)(2,1)}, u32[]{:S(2)}) copy-start(bf16[72,256]{1,0:T(8,128)(2,1)} %param.23) | copy-start | bytes 110596
  7.2 187.3 %all-gather.5.cloned.1.call-start = ((), (), s32[]{:S(2)}) async-start(), calls=%async_computation.7 | async-start | bytes 2506752 | tf_op jit(solution)/shard_map/all_gather | solution.py:97
  8.0 197.1 %all-gather.7.cloned.1.call-start = ((), (), s32[]{:S(2)}) async-start(), calls=%async_computation.8 | async-start | bytes 2506752 | tf_op jit(solution)/shard_map/all_gather | solution.py:100
  8.7 255.6 %all-gather.9.cloned.1.call-start = ((), (), s32[]{:S(2)}) async-start(), calls=%async_computation.9 | async-start | bytes 5013504 | tf_op jit(solution)/shard_map/all_gather | solution.py:154
  112.3 53.1 %copy-start.21 = (f32[128,256]{1,0:T(8,128)}, f32[128,256]{1,0:T(8,128)S(1)}, u32[]{:S(2)}) copy-start(f32[128,256]{1,0:T(8,128)S(1)} %get-tuple-element.73) | copy-start | bytes 393220
  112.5 86.5 %copy-start.40 = (f32[128]{0:T(128)}, f32[128]{0:T(128)S(1)}, u32[]{:S(2)}) copy-start(f32[128]{0:T(128)S(1)} %convert_bitcast_fusion.1) | copy-start | bytes 1540
  112.8 89.0 %copy-start.32 = (f32[128,128]{1,0:T(8,128)}, f32[128,128]{1,0:T(8,128)S(1)}, u32[]{:S(2)}) copy-start(f32[128,128]{1,0:T(8,128)S(1)} %get-tuple-element.66) | copy-start | bytes 196612
  112.9 89.0 %copy-start.34 = (f32[128,128]{1,0:T(8,128)}, f32[128,128]{1,0:T(8,128)S(1)}, u32[]{:S(2)}) copy-start(f32[128,128]{1,0:T(8,128)S(1)} %get-tuple-element.67) | copy-start | bytes 196612
  142.3 60.2 %copy-start.12 = (bf16[1024,256]{1,0:T(8,128)(2,1)}, bf16[1024,256]{1,0:T(8,128)(2,1)S(1)}, u32[]{:S(2)}) copy-start(bf16[1024,256]{1,0:T(8,128)(2,1)S(1)} %all_gather.47) | copy-start | bytes 1572868
  194.6 8.9 copy-start.36
  209.0 152.7 %reduce-scatter.8.cloned.1.call-start = ((), (), s32[]{:S(2)}) async-start(), calls=%async_computation.10 | async-start | bytes 5013504 | tf_op jit(solution)/shard_map/reduce_scatter | solution.py:159
  280.1 82.7 %copy-start.14 = (bf16[1,128,1152]{2,1,0:T(8,128)(2,1)S(1)}, bf16[1,128,1152]{2,1,0:T(8,128)(2,1)}, u32[]{:S(2)}) copy-start(bf16[1,128,1152]{2,1,0:T(8,128)(2,1)} %param.18) | copy-start | bytes 884740
  280.1 142.7 %all-gather.11.cloned.1.call-start = ((), (), s32[]{:S(2)}) async-start(), calls=%async_computation.11 | async-start | bytes 5013504 | tf_op jit(solution)/shard_map/all_gather | solution.py:170
  366.0 154.7 %reduce-scatter.10.cloned.1.call-start = ((), (), s32[]{:S(2)}) async-start(), calls=%async_computation.12 | async-start | bytes 5013504 | tf_op jit(solution)/shard_map/reduce_scatter | solution.py:177
  422.8 8.6 copy-start.45
  439.1 82.9 %copy-start.11 = (bf16[128,1152]{1,0:T(8,128)(2,1)S(1)}, bf16[128,1152]{1,0:T(8,128)(2,1)}, u32[]{:S(2)}) copy-start(bf16[128,1152]{1,0:T(8,128)(2,1)} %reduce-scatter.8.cloned.1.call-done) | copy-start | bytes 884740
  439.1 133.2 %reduce-scatter.12.cloned.1.call-start = ((), (), s32[]{:S(2)}) async-start(), calls=%async_computation.13 | async-start | bytes 1179648 | tf_op jit(solution)/shard_map/reduce_scatter | solution.py:205
  532.4 42.9 %copy-start.41 = (f32[128]{0:T(128)S(1)}, f32[128]{0:T(128)}, u32[]{:S(2)}) copy-start(f32[128]{0:T(128)} %copy-done.40) | copy-start | bytes 1540
  532.4 43.2 %copy-start.22 = (f32[128,256]{1,0:T(8,128)S(1)}, f32[128,256]{1,0:T(8,128)}, u32[]{:S(2)}) copy-start(f32[128,256]{1,0:T(8,128)} %copy-done.21) | copy-start | bytes 393220
  533.5 43.8 %copy-start.20 = (bf16[256,4,128]{2,0,1:T(8,128)(2,1)S(1)}, bf16[256,4,128]{2,0,1:T(8,128)(2,1)}, u32[]{:S(2)}) copy-start(bf16[256,4,128]{2,0,1:T(8,128)(2,1)} %copy-done.19) | copy-start | bytes 786436
  533.6 127.0 %reduce-scatter.18.cloned.1.call-start = ((), (), s32[]{:S(2)}) async-start(), calls=%async_computation.16 | async-start | bytes 626688 | tf_op jit(solution)/shard_map/reduce_scatter | solution.py:233
  574.4 131.6 %reduce-scatter.16.cloned.1.call-start = ((), (), s32[]{:S(2)}) async-start(), calls=%async_computation.15 | async-start | bytes 626688 | tf_op jit(solution)/shard_map/reduce_scatter | solution.py:230
  577.3 203.8 %reduce-scatter.20.cloned.1.call-start = ((), (), s32[]{:S(2)}) async-start(), calls=%async_computation.17 | async-start | bytes 2506752 | tf_op jit(solution)/shard_map/reduce_scatter | solution.py:236
  579.6 276.8 %reduce-scatter.14.cloned.1.call-start = ((), (), s32[]{:S(2)}) async-start(), calls=%async_computation.14 | async-start | bytes 2506752 | tf_op jit(solution)/shard_map/reduce_scatter | solution.py:227
  583.7 7.9 slice-start
  583.7 344.6 %all-reduce.19.cloned.1.call-start = ((), (), s32[]{:S(2)}) async-start(), calls=%async_computation.18 | async-start | bytes 153600 | tf_op jit(solution)/shard_map/psum | solution.py:260
  585.1 6.5 slice-start.1
  706.0 378.8 %all-reduce.21.cloned.1.call-start = ((), (), s32[]{:S(2)}) async-start(), calls=%async_computation.19 | async-start | bytes 6561792 | tf_op jit(solution)/shard_map/psum | solution.py:259
  712.3 144.1 %copy-start.10 = (f32[128,1152]{1,0:T(8,128)S(1)}, f32[128,1152]{1,0:T(8,128)}, u32[]{:S(2)}) copy-start(f32[128,1152]{1,0:T(8,128)} %copy-done.9) | copy-start | bytes 1769476
  (37 other events, 99.2 us)
Sparse Core Ops, SparseCore 0:
  10.5 51.5 all-gather.4
  64.5 49.3 all-gather.6
  209.1 55.2 all-gather.8
  280.3 81.4 reduce-scatter.7
  366.2 56.6 all-gather.10
  439.2 81.4 reduce-scatter.9
  533.7 38.5 reduce-scatter.11
  576.0 62.8 reduce-scatter.17
  642.6 63.2 reduce-scatter.15
  709.8 71.2 reduce-scatter.19
  785.0 71.2 reduce-scatter.13
  859.8 68.4 all-reduce.18
  932.1 152.6 all-reduce.20
where the time goes:
time: 1100 us
  waiting for transfers between devices  722 us (66%)
  blocking collectives  232 us (21%)
  matrix products  69.1 us (6%)
  other arithmetic  35.6 us (3%)
  local copies, waits for them, and re-layouts  22.2 us (2%)
  between operations  17.4 us (2%)
    psum x1, waiting for transfers between devices, body(): lax.psum(shards[0].astype(jnp.bfloat16), 'ctx').astype(jnp.float32)  147 us
    unnamed x2, blocking collectives  125 us
    reduce_scatter x1, waiting for transfers between devices, body(): lax.psum_scatter((jnp.dot(grad_gate, w_gate, preferred_element_type=f32)...  81.6 us
    reduce_scatter x1, waiting for transfers between devices, body(): lax.psum_scatter(jnp.dot(hidden, w_down, preferred_element_type=f32).asty...  81.5 us
    reduce_scatter x1, waiting for transfers between devices, body(): lax.psum_scatter(term_query.astype(jnp.bfloat16), 'fsdp', scatter_dimensi...  75.3 us
    psum x1, waiting for transfers between devices, body(): lax.psum(shards[1].astype(jnp.bfloat16), 'ctx').astype(jnp.float32)  71 us
    reduce_scatter x1, waiting for transfers between devices, body(): lax.psum_scatter(term_output.astype(jnp.bfloat16), 'fsdp', scatter_dimens...  68.7 us
    all_gather x1, waiting for transfers between devices, body(): grad_all = lax.all_gather(grad_ffn, 'fsdp', axis=0, tiled=True)  56.5 us
  transfers between devices with their start and end apart: 13, of which 10 were waited for; matrix products, arithmetic and copies ran while one was open for 5% of the time, Pallas kernels for 0%

commit v1 on v0

--- a/solution.py
+++ b/solution.py
@@ -95,7 +95,9 @@
     block = local // 2
     gathered = (
         lax.all_gather(w_query, "fsdp", axis=0, tiled=True),
-        lax.all_gather(w_key, "fsdp", axis=0, tiled=True),
+        jnp.concatenate(
+            lax.all_to_all(jnp.stack([w_key] * lax.axis_size("fsdp")), "fsdp", 0, 0), axis=0
+        ),
         lax.all_gather(w_value, "fsdp", axis=0, tiled=True),
         lax.all_gather(w_output, "fsdp", axis=1, tiled=True),
         lax.all_gather(gain_in, "fsdp", axis=0, tiled=True),

time: 1100 us -> 1080 us (0.982)
  blocking collectives: 232 us -> 209 us
    all_gather x1 -> x0, blocking collectives: 26.9 us -> none  [body(): lax.all_gather(w_key, 'fsdp', axis=0, tiled=True)]
  transfers between devices with their start and end apart: 13 -> 14, of which waited for: 10 -> 10; matrix products, arithmetic and copies ran while one was open for 5% -> 5% of each run, Pallas kernels for 0% -> 0%
where the time goes in v1:
time: 1080 us
  waiting for transfers between devices  723 us (67%)
  blocking collectives  209 us (19%)
  matrix products  67.9 us (6%)
  other arithmetic  36.5 us (3%)
  local copies, waits for them, and re-layouts  19.3 us (2%)
  between operations  17.5 us (2%)
    psum x1, waiting for transfers between devices, body(): lax.psum(shards[0].astype(jnp.bfloat16), 'ctx').astype(jnp.float32)  147 us
    unnamed x2, blocking collectives  124 us
    reduce_scatter x1, waiting for transfers between devices, body(): lax.psum_scatter((jnp.dot(grad_gate, w_gate, preferred_element_type=f32)...  81.6 us
    reduce_scatter x1, waiting for transfers between devices, body(): lax.psum_scatter(jnp.dot(hidden, w_down, preferred_element_type=f32).asty...  81.5 us
    reduce_scatter x1, waiting for transfers between devices, body(): lax.psum_scatter(term_query.astype(jnp.bfloat16), 'fsdp', scatter_dimensi...  75.3 us
    psum x1, waiting for transfers between devices, body(): lax.psum(shards[1].astype(jnp.bfloat16), 'ctx').astype(jnp.float32)  71.1 us
    reduce_scatter x1, waiting for transfers between devices, body(): lax.psum_scatter(term_output.astype(jnp.bfloat16), 'fsdp', scatter_dimens...  68.7 us
    all_gather x1, waiting for transfers between devices, body(): grad_all = lax.all_gather(grad_ffn, 'fsdp', axis=0, tiled=True)  56.5 us
  transfers between devices with their start and end apart: 14, of which 10 were waited for; matrix products, arithmetic and copies ran while one was open for 5% of the time, Pallas kernels for 0%

profile of v1, /device:TPU:8, one launch (start us, length us, event | category | flops | bytes accessed | tf_op | source)
XLA Modules:
  0.0 1082.4 jit_solution(5077661041885405316)
XLA Ops:
  9.6 8.2 all-to-all-start
  24.9 64.5 %all-reduce.13 = (bf16[1152]{0:T(1024)(128)(2,1)S(1)}, bf16[256]{0:T(256)(128)(2,1)S(1)}, bf16[256]{0:T(256)(128)(2,1)S(1)}, bf16[1152]{0:T(1024)(128)(2,1)S(1)}...) all-reduce(bf16[1152]{0:T(1024)(128)(2,1)S(1)} %dynamic-update-slic, ...), channel_id=1, replica_groups=mesh['ctx'=8,'fsdp'=16] {'fsdp'}, use_global_device_ids=true, to_apply=%add | all-reduce | flops 5120 | bytes 20480
  89.8 26.5 %all_gather.40 = bf16[1152,256]{1,0:T(8,128)(2,1)S(1)} all-gather(bf16[72,256]{1,0:T(8,128)(2,1)S(1)} %copy-done.39), channel_id=1, replica_groups=mesh['ctx'=8,'fsdp'=16] {'fsdp'}, dimensions={0}, use_global_device_ids=true | all-gather | bytes 626688 | tf_op jit(solution)/shard_map/all_gather | solution.py:101
  117.1 29.3 %all_gather.41 = bf16[1024,256]{1,0:T(8,128)(2,1)S(1)} all-gather(bf16[128,256]{1,0:T(8,128)(2,1)S(1)} %convolution_convert_fusion.10), channel_id=1, replica_groups=mesh['ctx'=8,'fsdp'=16] {'ctx'}, dimensions={0}, use_global_device_ids=true | all-gather | bytes 589824 | tf_op jit(solution)/shard_map/all_gather | solution.py:137
  147.3 28.9 %all_gather.43 = bf16[1024,256]{1,0:T(8,128)(2,1)S(1)} all-gather(bf16[128,256]{1,0:T(8,128)(2,1)S(1)} %pad_maximum_fusion.3), channel_id=1, replica_groups=mesh['ctx'=8,'fsdp'=16] {'ctx'}, dimensions={0}, use_global_device_ids=true | all-gather | bytes 589824 | tf_op jit(solution)/shard_map/all_gather | solution.py:136
  176.2 4.5 copy.77
  180.7 2.6 multiply_reduce_fusion.7
  186.8 2.7 multiply_reduce_fusion.3
  190.9 55.7 %all-gather.9.cloned.1.call-done = bf16[2048,1152]{1,0:T(8,128)(2,1)} async-done(((bf16[128,1152]{1,0:T(8,128)(2,1)}), bf16[2048,1152]{1,0:T(8,128)(2,1)}) %all-gather.9.cloned.1.call-update) | async-done | bytes 4718608 | tf_op jit(solution)/shard_map/all_gather | solution.py:156
  246.6 5.3 fusion.103
  251.9 4.6 multiply_convert_fusion.1
  257.7 4.7 convolution_convert_fusion
  262.5 81.5 %reduce-scatter.8.cloned.1.call-done = bf16[128,1152]{1,0:T(8,128)(2,1)} async-done(((bf16[2048,1152]{1,0:T(8,128)(2,1)}), bf16[128,1152]{1,0:T(8,128)(2,1)}) %reduce-scatter.8.cloned.1.call-update) | async-done | bytes 294928 | tf_op jit(solution)/shard_map/reduce_scatter | solution.py:161
  348.6 56.5 %all-gather.11.cloned.1.call-done = bf16[2048,1152]{1,0:T(8,128)(2,1)} async-done(((bf16[128,1152]{1,0:T(8,128)(2,1)}), bf16[2048,1152]{1,0:T(8,128)(2,1)}) %all-gather.11.cloned.1.call-update) | async-done | bytes 4718608 | tf_op jit(solution)/shard_map/all_gather | solution.py:172
  405.1 8.5 multiply_convert_fusion
  413.7 3.0 fusion.104
  416.7 4.6 add_convert_fusion
  421.4 81.6 %reduce-scatter.10.cloned.1.call-done = bf16[128,1152]{1,0:T(8,128)(2,1)} async-done(((bf16[2048,1152]{1,0:T(8,128)(2,1)}), bf16[128,1152]{1,0:T(8,128)(2,1)}) %reduce-scatter.10.cloned.1.call-update) | async-done | bytes 294928 | tf_op jit(solution)/shard_map/reduce_scatter | solution.py:179
  504.2 2.3 multiply_reduce_fusion
  515.8 38.5 %reduce-scatter.12.cloned.1.call-done = bf16[128,512]{1,0:T(8,128)(2,1)} async-done(((bf16[1024,512]{1,0:T(8,128)(2,1)}), bf16[128,512]{1,0:T(8,128)(2,1)}) %reduce-scatter.12.cloned.1.call-update) | async-done | bytes 131088 | tf_op jit(solution)/shard_map/reduce_scatter | solution.py:207
  559.5 2.2 convolution_convert_fusion.1
  563.5 2.3 convolution_convert_fusion.2
  567.3 6.5 convolution_convert_fusion.3
  573.8 3.4 convolution_convert_fusion.4
  579.1 59.8 %all-reduce.12 = (bf16[1152]{0:T(1024)(128)(2,1)S(1)}, bf16[256]{0:T(256)(128)(2,1)S(1)}, bf16[256]{0:T(256)(128)(2,1)S(1)}, bf16[1152]{0:T(1024)(128)(2,1)S(1)}...) all-reduce(bf16[1152]{0:T(1024)(128)(2,1)S(1)} %get-tuple-element.2, ...), channel_id=9, replica_groups=mesh['ctx'=8,'fsdp'=16] {'fsdp'}, use_global_device_ids=true, to_apply=%region_32.33.clone | all-reduce | flops 5120 | bytes 20480
  642.4 45.7 %reduce-scatter.16.cloned.1.call-done = bf16[72,256]{1,0:T(8,128)(2,1)} async-done(((bf16[1152,256]{1,0:T(8,128)(2,1)}), bf16[72,256]{1,0:T(8,128)(2,1)}) %reduce-scatter.16.cloned.1.call-update) | async-done | bytes 36880 | tf_op jit(solution)/shard_map/reduce_scatter | solution.py:232
  688.2 6.3 convolution_convert_fusion.5
  694.5 68.7 %reduce-scatter.20.cloned.1.call-done = bf16[1024,72]{0,1:T(8,128)(2,1)} async-done(((bf16[1024,1152]{0,1:T(8,128)(2,1)}), bf16[1024,72]{0,1:T(8,128)(2,1)}) %reduce-scatter.20.cloned.1.call-update) | async-done | bytes 147472 | tf_op jit(solution)/shard_map/reduce_scatter | solution.py:238
  763.2 75.3 %reduce-scatter.14.cloned.1.call-done = bf16[72,1024]{1,0:T(8,128)(2,1)} async-done(((bf16[1152,1024]{1,0:T(8,128)(2,1)}), bf16[72,1024]{1,0:T(8,128)(2,1)}) %reduce-scatter.14.cloned.1.call-update) | async-done | bytes 147472 | tf_op jit(solution)/shard_map/reduce_scatter | solution.py:229
  839.5 71.1 %all-reduce.19.cloned.1.call-done = (bf16[72,256]{1,0:T(8,128)(2,1)}, bf16[72,256]{1,0:T(8,128)(2,1)}, bf16[72]{0:T(256)(128)(2,1)}, bf16[16]{0:T(256)(128)(2,1)...) async-done(((bf16[72,256]{1,0:T(8,128)(2,1)}, bf16[72,256]{1,0:T(8,128)(2,1)}, bf16[72]{0:T(256)(128)(2,1)}, ...) | async-done | bytes 74384 | tf_op jit(solution)/shard_map/psum | solution.py:262
  920.4 146.6 %all-reduce.21.cloned.1.call-done = (bf16[72,1024]{1,0:T(8,128)(2,1)}, bf16[1024,72]{0,1:T(8,128)(2,1)}, bf16[432,1152]{1,0:T(8,128)(2,1)}, bf16[432,1152]{1,0:T(8,128)(2,1)}, bf16[432,1152]{1,0:T(8,128)(2,1)}) async-done(((bf16[72,1024]{1,0:T(8,128)(2,1)}, bf16[1024,72]{0,1:T(8,128)(2,1)}, bf16[432,1152]{1,0:T(8,128)(2,1)}, bf16[432,1152]{1,0:T(8,128)(2,1)}, bf16[432,1152]{1,0:T(8,128)(2,1)}), ...) | async-done | bytes 3280912 | tf_op jit(solution)/shard_map/psum | solution.py:261
  1070.4 2.7 convert_element_type.289
  (257 shorter events, 60.3 us)
Async XLA Ops:
  7.2 250.5 %copy-start = (bf16[432,1152]{1,0:T(8,128)(2,1)S(1)}, bf16[432,1152]{1,0:T(8,128)(2,1)}, u32[]{:S(2)}) copy-start(bf16[432,1152]{1,0:T(8,128)(2,1)} %param.27) | copy-start | bytes 2985988
  7.2 109.1 %copy-start.2 = (bf16[1,128,1152]{2,1,0:T(8,128)(2,1)S(1)}, bf16[1,128,1152]{2,1,0:T(8,128)(2,1)}, u32[]{:S(2)}) copy-start(bf16[1,128,1152]{2,1,0:T(8,128)(2,1)} %param.17) | copy-start | bytes 884740
  7.2 16.7 %copy-start.51 = (bf16[72]{0:T(256)(128)(2,1)S(1)}, bf16[72]{0:T(256)(128)(2,1)}, u32[]{:S(2)}) copy-start(bf16[72]{0:T(256)(128)(2,1)} %param.32) | copy-start | bytes 436
  7.3 16.9 %copy-start.52 = (bf16[72]{0:T(256)(128)(2,1)S(1)}, bf16[72]{0:T(256)(128)(2,1)}, u32[]{:S(2)}) copy-start(bf16[72]{0:T(256)(128)(2,1)} %param.31) | copy-start | bytes 436
  7.3 17.2 %copy-start.53 = (bf16[72]{0:T(256)(128)(2,1)S(1)}, bf16[72]{0:T(256)(128)(2,1)}, u32[]{:S(2)}) copy-start(bf16[72]{0:T(256)(128)(2,1)} %param.28) | copy-start | bytes 436
  7.3 17.4 %copy-start.54 = (bf16[72]{0:T(256)(128)(2,1)S(1)}, bf16[72]{0:T(256)(128)(2,1)}, u32[]{:S(2)}) copy-start(bf16[72]{0:T(256)(128)(2,1)} %param.33) | copy-start | bytes 436
  7.3 82.5 %copy-start.39 = (bf16[72,256]{1,0:T(8,128)(2,1)S(1)}, bf16[72,256]{1,0:T(8,128)(2,1)}, u32[]{:S(2)}) copy-start(bf16[72,256]{1,0:T(8,128)(2,1)} %param.23) | copy-start | bytes 110596
  7.3 168.9 %all-gather.5.cloned.1.call-start = ((), (), s32[]{:S(2)}) async-start(), calls=%async_computation.8 | async-start | bytes 2506752 | tf_op jit(solution)/shard_map/all_gather | solution.py:97
  9.6 136.7 %all-to-all-start = ((bf16[16,72,256]{2,1,0:T(8,128)(2,1)}), bf16[16,72,256]{2,1,0:T(8,128)(2,1)S(1)}, u32[]{:S(2)}, u32[]{:S(2)}) async-start(bf16[16,72,256]{2,1,0:T(8,128)(2,1)} %stack.2), calls=%async_computation | async-start | bytes 1179648 | tf_op jit(solution)/shard_map/all_to_all | solution.py:99
  17.9 168.9 %all-gather.7.cloned.1.call-start = ((), (), s32[]{:S(2)}) async-start(), calls=%async_computation.9 | async-start | bytes 2506752 | tf_op jit(solution)/shard_map/all_gather | solution.py:102
  18.6 227.9 %all-gather.9.cloned.1.call-start = ((), (), s32[]{:S(2)}) async-start(), calls=%async_computation.10 | async-start | bytes 5013504 | tf_op jit(solution)/shard_map/all_gather | solution.py:156
  116.3 64.4 %copy-start.40 = (f32[128]{0:T(128)}, f32[128]{0:T(128)S(1)}, u32[]{:S(2)}) copy-start(f32[128]{0:T(128)S(1)} %multiply_power_fusion) | copy-start | bytes 1540
  146.4 38.8 %copy-start.36 = (bf16[1024,256]{1,0:T(8,128)(2,1)}, bf16[1024,256]{1,0:T(8,128)(2,1)S(1)}, u32[]{:S(2)}) copy-start(bf16[1024,256]{1,0:T(8,128)(2,1)S(1)} %all_gather.41) | copy-start | bytes 1572868
  146.8 34.0 %copy-start.21 = (f32[128,256]{1,0:T(8,128)}, f32[128,256]{1,0:T(8,128)S(1)}, u32[]{:S(2)}) copy-start(f32[128,256]{1,0:T(8,128)S(1)} %get-tuple-element.73) | copy-start | bytes 393220
  147.2 36.3 %copy-start.32 = (f32[128,128]{1,0:T(8,128)}, f32[128,128]{1,0:T(8,128)S(1)}, u32[]{:S(2)}) copy-start(f32[128,128]{1,0:T(8,128)S(1)} %get-tuple-element.66) | copy-start | bytes 196612
  147.2 36.3 %copy-start.34 = (f32[128,128]{1,0:T(8,128)}, f32[128,128]{1,0:T(8,128)S(1)}, u32[]{:S(2)}) copy-start(f32[128,128]{1,0:T(8,128)S(1)} %get-tuple-element.67) | copy-start | bytes 196612
  190.7 153.3 %reduce-scatter.8.cloned.1.call-start = ((), (), s32[]{:S(2)}) async-start(), calls=%async_computation.11 | async-start | bytes 5013504 | tf_op jit(solution)/shard_map/reduce_scatter | solution.py:161
  262.4 82.7 %copy-start.14 = (bf16[1,128,1152]{2,1,0:T(8,128)(2,1)S(1)}, bf16[1,128,1152]{2,1,0:T(8,128)(2,1)}, u32[]{:S(2)}) copy-start(bf16[1,128,1152]{2,1,0:T(8,128)(2,1)} %param.18) | copy-start | bytes 884740
  262.4 142.7 %all-gather.11.cloned.1.call-start = ((), (), s32[]{:S(2)}) async-start(), calls=%async_computation.12 | async-start | bytes 5013504 | tf_op jit(solution)/shard_map/all_gather | solution.py:172
  348.3 154.6 %reduce-scatter.10.cloned.1.call-start = ((), (), s32[]{:S(2)}) async-start(), calls=%async_computation.13 | async-start | bytes 5013504 | tf_op jit(solution)/shard_map/reduce_scatter | solution.py:179
  421.3 82.9 %copy-start.11 = (bf16[128,1152]{1,0:T(8,128)(2,1)S(1)}, bf16[128,1152]{1,0:T(8,128)(2,1)}, u32[]{:S(2)}) copy-start(bf16[128,1152]{1,0:T(8,128)(2,1)} %reduce-scatter.8.cloned.1.call-done) | copy-start | bytes 884740
  421.3 133.0 %reduce-scatter.12.cloned.1.call-start = ((), (), s32[]{:S(2)}) async-start(), calls=%async_computation.14 | async-start | bytes 1179648 | tf_op jit(solution)/shard_map/reduce_scatter | solution.py:207
  514.6 42.8 %copy-start.41 = (f32[128]{0:T(128)S(1)}, f32[128]{0:T(128)}, u32[]{:S(2)}) copy-start(f32[128]{0:T(128)} %copy-done.40) | copy-start | bytes 1540
  514.7 43.1 %copy-start.22 = (f32[128,256]{1,0:T(8,128)S(1)}, f32[128,256]{1,0:T(8,128)}, u32[]{:S(2)}) copy-start(f32[128,256]{1,0:T(8,128)} %copy-done.21) | copy-start | bytes 393220
  515.8 43.7 %copy-start.20 = (bf16[256,4,128]{2,0,1:T(8,128)(2,1)S(1)}, bf16[256,4,128]{2,0,1:T(8,128)(2,1)}, u32[]{:S(2)}) copy-start(bf16[256,4,128]{2,0,1:T(8,128)(2,1)} %copy-done.19) | copy-start | bytes 786436
  515.8 126.7 %reduce-scatter.18.cloned.1.call-start = ((), (), s32[]{:S(2)}) async-start(), calls=%async_computation.17 | async-start | bytes 626688 | tf_op jit(solution)/shard_map/reduce_scatter | solution.py:235
  556.5 131.6 %reduce-scatter.16.cloned.1.call-start = ((), (), s32[]{:S(2)}) async-start(), calls=%async_computation.16 | async-start | bytes 626688 | tf_op jit(solution)/shard_map/reduce_scatter | solution.py:232
  559.4 203.8 %reduce-scatter.20.cloned.1.call-start = ((), (), s32[]{:S(2)}) async-start(), calls=%async_computation.18 | async-start | bytes 2506752 | tf_op jit(solution)/shard_map/reduce_scatter | solution.py:238
  561.7 276.7 %reduce-scatter.14.cloned.1.call-start = ((), (), s32[]{:S(2)}) async-start(), calls=%async_computation.15 | async-start | bytes 2506752 | tf_op jit(solution)/shard_map/reduce_scatter | solution.py:229
  565.9 344.7 %all-reduce.19.cloned.1.call-start = ((), (), s32[]{:S(2)}) async-start(), calls=%async_computation.19 | async-start | bytes 153600 | tf_op jit(solution)/shard_map/psum | solution.py:262
  688.1 378.8 %all-reduce.21.cloned.1.call-start = ((), (), s32[]{:S(2)}) async-start(), calls=%async_computation.20 | async-start | bytes 6561792 | tf_op jit(solution)/shard_map/psum | solution.py:261
  694.5 144.1 %copy-start.10 = (f32[128,1152]{1,0:T(8,128)S(1)}, f32[128,1152]{1,0:T(8,128)}, u32[]{:S(2)}) copy-start(f32[128,1152]{1,0:T(8,128)} %copy-done.9) | copy-start | bytes 1769476
  (44 other events, 177.6 us)
Sparse Core Ops, SparseCore 0:
  10.6 52.4 all-gather.4
  65.5 48.7 all-gather.6
  190.8 55.7 all-gather.8
  262.5 81.4 reduce-scatter.7
  348.4 56.6 all-gather.10
  421.5 81.4 reduce-scatter.9
  515.9 38.4 reduce-scatter.11
  558.1 62.8 reduce-scatter.17
  624.8 63.3 reduce-scatter.15
  691.9 71.2 reduce-scatter.19
  767.2 71.2 reduce-scatter.13
  842.0 68.5 all-reduce.18
  914.3 152.6 all-reduce.20
